TPU v7x, 768 devices: a whole 4x8x12 slice. The times are simulated.
768 devices in a mesh: blk: 24 (over x, z_hi, core), sub: 32 (over z_lo, y).
Axes of the slice: x: 4, y: 8, z: 12 (z_hi: 3, z_lo: 4; z = z_hi * 4 + z_lo), core: 2. Of those that a mesh axis runs over, the one named last changes fastest.
Arguments:
- images: bfloat16 [393216, 768], P(('blk', 'sub')), may hold values from -6 to 6
- texts: bfloat16 [393216, 768], P(('blk', 'sub')), may hold values from -6 to 6
- logit_scale: float32 [1], replicated, may hold values from 2 to 10
- logit_bias: float32 [1], replicated, may hold values from -4 to -1
Outputs:
- grad_images: float32 [393216, 768], P(('blk', 'sub'))
- grad_texts: float32 [393216, 768], P(('blk', 'sub'))
All inputs are finite; a program needn't handle non-finite values.
Results may differ from a plain program's by a relative error of at most 0.004.
Values may be sent and summed in bfloat16 or wider, within the bound.
A program may use at most 32 MiB of HBM per device.

v0:
```python
import jax
import jax.numpy as jnp
from jax import lax
from jax.sharding import PartitionSpec as P


def passed_along(value, axis, steps):
    count = lax.axis_size(axis)
    pairs = [(source, (source + steps) % count) for source in range(count)]
    return lax.ppermute(value, axis, pairs)


def unit_rows(values_in):
    values = values_in.astype(jnp.float32)
    recip = lax.rsqrt(jnp.sum(values * values, axis=-1, keepdims=True) + 1e-06)
    return (values * recip, recip)


def tile_weights(left, right, scale, offset):
    logits = (
        scale
        * lax.dot_general(left, right, (((1,), (1,)), ((), ())), preferred_element_type=jnp.float32)
        + offset
    )
    return jax.nn.sigmoid(logits)


def contract_rows(weights, rows):
    return lax.dot_general(
        weights, rows, (((0,), (0,)), ((), ())), preferred_element_type=jnp.float32
    )


def back_norm(unit, recip, grad):
    return (grad - unit * jnp.sum(unit * grad, axis=-1, keepdims=True)) * recip


def shards(images, texts, logit_scale, logit_bias):
    unit_img, recip_img = unit_rows(images)
    unit_txt, recip_txt = unit_rows(texts)
    img_low = unit_img.astype(jnp.bfloat16)
    txt_low = unit_txt.astype(jnp.bfloat16)
    scale = logit_scale[0]
    offset = logit_bias[0]
    diagonal_one = jnp.eye(images.shape[0], dtype=jnp.float32)
    weight_own = (tile_weights(img_low, txt_low, scale, offset) - diagonal_one).astype(jnp.bfloat16)
    img_prev, txt_prev = passed_along((img_low, txt_low), ("blk", "sub"), 1)
    img_next, txt_next = passed_along((img_low, txt_low), ("blk", "sub"), -1)
    weight_prev = tile_weights(img_low, txt_prev, scale, offset).astype(jnp.bfloat16)
    weight_next = tile_weights(img_low, txt_next, scale, offset).astype(jnp.bfloat16)
    from_prev = tile_weights(img_prev, txt_low, scale, offset).astype(jnp.bfloat16)
    from_next = tile_weights(img_next, txt_low, scale, offset).astype(jnp.bfloat16)
    grad_txt = scale * (
        contract_rows(weight_own, img_low)
        + contract_rows(from_prev, img_prev)
        + contract_rows(from_next, img_next)
    )
    grad_img = scale * (
        jnp.dot(weight_own, txt_low, preferred_element_type=jnp.float32)
        + jnp.dot(weight_prev, txt_prev, preferred_element_type=jnp.float32)
        + jnp.dot(weight_next, txt_next, preferred_element_type=jnp.float32)
    )
    return (back_norm(unit_img, recip_img, grad_img), back_norm(unit_txt, recip_txt, grad_txt))


def solution(mesh):
    in_specs = (P(("blk", "sub"), None), P(("blk", "sub"), None), P(), P())
    out_specs = (P(("blk", "sub"), None), P(("blk", "sub"), None))
    return jax.shard_map(shards, mesh=mesh, in_specs=in_specs, out_specs=out_specs, check_vma=False)
```

profile of v0, /device:TPU:6, one launch (start us, length us, event | category | flops | bytes accessed | tf_op | source)
XLA Modules:
  0.0 70.0 jit_solution(6604315384522200199)
XLA Ops:
  0.6 0.0 copy-start
  0.6 1.4 %fusion.13 = f32[512]{0:T(512)S(1)} fusion(bf16[512,768]{1,0:T(8,128)(2,1)} %param.5), kind=kLoop, calls=%fused_computation.17 | loop fusion | flops 1179136 | bytes 788480 | tf_op jit(solution)/shard_map/reduce_sum | solution.py:15
  2.1 2.2 %fusion.2 = bf16[512,768]{1,0:T(8,128)(2,1)} fusion(bf16[512,768]{1,0:T(8,128)(2,1)} %param.5, f32[512]{0:T(512)S(1)} %add_rsqrt_fusion), kind=kLoop, calls=%fused_computation.4 | loop fusion | flops 1179648 | bytes 1574912 | tf_op jit(solution)/shard_map/convert_element_type | solution.py:42
  4.3 17.3 %collective-permute-start.1 = (bf16[512,768]{1,0:T(8,128)(2,1)}, bf16[512,768]{1,0:T(8,128)(2,1)}, u32[]{:S(2)}, u32[]{:S(2)}) collective-permute-start(bf16[512,768]{1,0:T(8,128)(2,1)} %fusion.2), channel_id=1, source_target_pairs={{0,767},{1,0},{2,1},{3,2},{4,3},{5,4},{6,5},{7,6},{8,7},{9,8},{10,... | collective-permute-start | bytes 2359304 | tf_op jit(solution)/shard_map/ppermute | solution.py:10
  21.6 1.9 %collective-permute-start = (bf16[512,768]{1,0:T(8,128)(2,1)}, bf16[512,768]{1,0:T(8,128)(2,1)}, u32[]{:S(2)}, u32[]{:S(2)}) collective-permute-start(bf16[512,768]{1,0:T(8,128)(2,1)} %fusion.2), channel_id=1, source_target_pairs={{0,1},{1,2},{2,3},{3,4},{4,5},{5,6},{6,7},{7,8},{8,9},{9,10},{10,1... | collective-permute-start | bytes 2359304 | tf_op jit(solution)/shard_map/ppermute | solution.py:10
  23.5 0.0 copy-done
  23.6 0.2 fusion.9
  23.8 1.1 %fusion.5 = bf16[512,768]{1,0:T(8,128)(2,1)} fusion(bf16[512,768]{1,0:T(8,128)(2,1)S(1)} %copy-done, f32[512]{0:T(512)S(1)} %add_rsqrt_fusion.1), kind=kLoop, calls=%fused_computation.9 | loop fusion | flops 1179648 | bytes 1574912 | tf_op jit(solution)/shard_map/convert_element_type | solution.py:41
  24.9 7.8 %collective-permute-start.3 = (bf16[512,768]{1,0:T(8,128)(2,1)}, bf16[512,768]{1,0:T(8,128)(2,1)}, u32[]{:S(2)}, u32[]{:S(2)}) collective-permute-start(bf16[512,768]{1,0:T(8,128)(2,1)} %fusion.5), channel_id=1, source_target_pairs={{0,767},{1,0},{2,1},{3,2},{4,3},{5,4},{6,5},{7,6},{8,7},{9,8},{10,... | collective-permute-start | bytes 2359304 | tf_op jit(solution)/shard_map/ppermute | solution.py:10
  32.7 1.9 %collective-permute-start.2 = (bf16[512,768]{1,0:T(8,128)(2,1)}, bf16[512,768]{1,0:T(8,128)(2,1)}, u32[]{:S(2)}, u32[]{:S(2)}) collective-permute-start(bf16[512,768]{1,0:T(8,128)(2,1)} %fusion.5), channel_id=1, source_target_pairs={{0,1},{1,2},{2,3},{3,4},{4,5},{5,6},{6,7},{7,8},{8,9},{9,10},{10,1... | collective-permute-start | bytes 2359304 | tf_op jit(solution)/shard_map/ppermute | solution.py:10
  36.0 0.0 copy-done.1
  36.0 0.8 %fusion.40 = bf16[512,512]{1,0:T(8,128)(2,1)S(1)} fusion(f32[]{:T(128)} %bitcast.17, f32[]{:T(128)} %bitcast.13, bf16[512,768]{1,0:T(8,128)(2,1)S(1)} %copy-done, f32[512]{0:T(512)S(1)} %add_rsqrt_fusion.1, bf16[512,768]{1,0:T(8,128)(2,1)S(1)} %copy-done.1, f32[512]{0:T(512)S(1)} %add_rsqrt_fusion), kind=kOutput, calls=%fused_computation.51 | convolution fusion | flops 407371776 | bytes 2101256 | tf_op jit(solution)/shard_map/dot_general | solution.py:22
  36.8 1.9 %fusion.74 = f32[512,768]{1,0:T(8,128)} fusion(bf16[512,512]{1,0:T(8,128)(2,1)S(1)} %fusion.40, bf16[512,768]{1,0:T(8,128)(2,1)S(1)} %copy-done.1, f32[512]{0:T(512)S(1)} %add_rsqrt_fusion), kind=kOutput, calls=%fused_computation.78 | convolution fusion | flops 403832832 | bytes 2885632 | tf_op jit(solution)/shard_map/dot_general | solution.py:59
  38.7 0.7 fusion.63
  39.4 7.3 %collective-permute-done = bf16[512,768]{1,0:T(8,128)(2,1)} collective-permute-done((bf16[512,768]{1,0:T(8,128)(2,1)}, bf16[512,768]{1,0:T(8,128)(2,1)}, u32[]{:S(2)}, u32[]{:S(2)}) %collective-permute-start) | collective-permute-done | bytes 786464 | tf_op jit(solution)/shard_map/ppermute | solution.py:10
  46.6 3.7 %fusion.45 = f32[512,768]{1,0:T(8,128)} fusion(bf16[512,768]{1,0:T(8,128)(2,1)} %collective-permute-done, f32[]{:T(128)} %bitcast.21, f32[]{:T(128)} %bitcast.16, bf16[512,768]{1,0:T(8,128)(2,1)S(1)} %copy-done, f32[512]{0:T(512)S(1)} %add_rsqrt_fusion.1), kind=kOutput, calls=%fused_computation.56 | convolution fusion | flops 808058880 | bytes 3147784 | tf_op jit(solution)/shard_map/dot_general | solution.py:60
  50.3 0.0 collective-permute-done.1
  50.3 4.7 %fusion.6 = (f32[512]{0:T(512)S(1)}, f32[512,768]{1,0:T(8,128)}) fusion(bf16[512,768]{1,0:T(8,128)(2,1)S(1)} %copy-done, f32[512]{0:T(512)S(1)} %add_rsqrt_fusion.1, bf16[512,768]{1,0:T(8,128)(2,1)} %collective-permute-done.1, f32[]{:T(128)} %bitcast.20, f32[]{:T(128)} %bitcast.12, f32[512,768]{1,0:T(8,128)} %fusion.74, f32[512,768]{1,0:T(8,128)} %fusion.45), kind=kOutput, calls=%fused_computation.10 | convolution fusion | flops 810810880 | bytes 6295560 | tf_op jit(solution)/shard_map/dot_general | solution.py:61
  55.0 2.9 %fusion.8 = f32[512,768]{1,0:T(8,128)} fusion(f32[512,768]{1,0:T(8,128)} %get-tuple-element.3, bf16[512,768]{1,0:T(8,128)(2,1)S(1)} %copy-done, f32[512]{0:T(512)S(1)} %get-tuple-element.2, f32[512]{0:T(512)S(1)} %add_rsqrt_fusion.1), kind=kLoop, calls=%fused_computation.12 | loop fusion | flops 1966080 | bytes 3936256 | tf_op jit(solution)/shard_map/mul | solution.py:35
  57.9 0.7 collective-permute-done.2
  58.6 3.9 %fusion.46 = f32[512,768]{1,0:T(8,128)} fusion(bf16[512,768]{1,0:T(8,128)(2,1)} %collective-permute-done.2, f32[]{:T(128)} %bitcast.19, f32[]{:T(128)} %bitcast.15, bf16[512,768]{1,0:T(8,128)(2,1)S(1)} %copy-done.1, f32[512]{0:T(512)S(1)} %add_rsqrt_fusion), kind=kOutput, calls=%fused_computation.57 | convolution fusion | flops 808058880 | bytes 3147784 | tf_op jit(solution)/shard_map/dot_general | solution.py:29
  62.5 0.0 collective-permute-done.3
  62.5 4.6 %fusion.10 = (f32[512]{0:T(512)S(1)}, f32[512,768]{1,0:T(8,128)}) fusion(bf16[512,768]{1,0:T(8,128)(2,1)S(1)} %copy-done.1, f32[512]{0:T(512)S(1)} %add_rsqrt_fusion, bf16[512,768]{1,0:T(8,128)(2,1)} %collective-permute-done.3, f32[]{:T(128)} %bitcast.18, f32[]{:T(128)} %bitcast.14, f32[512,768]{1,0:T(8,128)S(1)} %fusion.63, f32[512,768]{1,0:T(8,128)} %fusion.46), kind=kOutput, calls=%fused_computation.14 | convolution fusion | flops 810810880 | bytes 6295560 | tf_op jit(solution)/shard_map/dot_general | solution.py:29
  67.1 2.9 %fusion.12 = f32[512,768]{1,0:T(8,128)} fusion(f32[512,768]{1,0:T(8,128)} %get-tuple-element.5, bf16[512,768]{1,0:T(8,128)(2,1)S(1)} %copy-done.1, f32[512]{0:T(512)S(1)} %get-tuple-element.4, f32[512]{0:T(512)S(1)} %add_rsqrt_fusion), kind=kLoop, calls=%fused_computation.16 | loop fusion | flops 1966080 | bytes 3936256 | tf_op jit(solution)/shard_map/mul | solution.py:35
  (3 shorter events, 0.0 us)
Async XLA Ops:
  0.6 22.9 %copy-start = (bf16[512,768]{1,0:T(8,128)(2,1)S(1)}, bf16[512,768]{1,0:T(8,128)(2,1)}, u32[]{:S(2)}) copy-start(bf16[512,768]{1,0:T(8,128)(2,1)} %param.4) | copy-start | bytes 2359300
  4.3 31.7 %copy-start.1 = (bf16[512,768]{1,0:T(8,128)(2,1)S(1)}, bf16[512,768]{1,0:T(8,128)(2,1)}, u32[]{:S(2)}) copy-start(bf16[512,768]{1,0:T(8,128)(2,1)} %param.5) | copy-start | bytes 2359300
  4.3 46.0 %collective-permute-start.1 = (bf16[512,768]{1,0:T(8,128)(2,1)}, bf16[512,768]{1,0:T(8,128)(2,1)}, u32[]{:S(2)}, u32[]{:S(2)}) collective-permute-start(bf16[512,768]{1,0:T(8,128)(2,1)} %fusion.2), channel_id=1, source_target_pairs={{0,767},{1,0},{2,1},{3,2},{4,3},{5,4},{6,5},{7,6},{8,7},{9,8},{10,... | collective-permute-start | bytes 2359304 | tf_op jit(solution)/shard_map/ppermute | solution.py:10
  21.6 25.0 %collective-permute-start = (bf16[512,768]{1,0:T(8,128)(2,1)}, bf16[512,768]{1,0:T(8,128)(2,1)}, u32[]{:S(2)}, u32[]{:S(2)}) collective-permute-start(bf16[512,768]{1,0:T(8,128)(2,1)} %fusion.2), channel_id=1, source_target_pairs={{0,1},{1,2},{2,3},{3,4},{4,5},{5,6},{6,7},{7,8},{8,9},{9,10},{10,1... | collective-permute-start | bytes 2359304 | tf_op jit(solution)/shard_map/ppermute | solution.py:10
  24.9 37.7 %collective-permute-start.3 = (bf16[512,768]{1,0:T(8,128)(2,1)}, bf16[512,768]{1,0:T(8,128)(2,1)}, u32[]{:S(2)}, u32[]{:S(2)}) collective-permute-start(bf16[512,768]{1,0:T(8,128)(2,1)} %fusion.5), channel_id=1, source_target_pairs={{0,767},{1,0},{2,1},{3,2},{4,3},{5,4},{6,5},{7,6},{8,7},{9,8},{10,... | collective-permute-start | bytes 2359304 | tf_op jit(solution)/shard_map/ppermute | solution.py:10
  32.7 25.8 %collective-permute-start.2 = (bf16[512,768]{1,0:T(8,128)(2,1)}, bf16[512,768]{1,0:T(8,128)(2,1)}, u32[]{:S(2)}, u32[]{:S(2)}) collective-permute-start(bf16[512,768]{1,0:T(8,128)(2,1)} %fusion.5), channel_id=1, source_target_pairs={{0,1},{1,2},{2,3},{3,4},{4,5},{5,6},{6,7},{7,8},{8,9},{9,10},{10,1... | collective-permute-start | bytes 2359304 | tf_op jit(solution)/shard_map/ppermute | solution.py:10
where the time goes:
time: 70.4 us; the launch traced here: 70 us
  starting transfers between devices  29 us (41%)
  matrix products  20.3 us (29%)
  other arithmetic  10.7 us (15%)
  waiting for transfers between devices  7.94 us (11%)
  between operations  2 us (3%)
    ppermute x4, starting transfers between devices, passed_along(): return lax.ppermute(value, axis, pairs)  29 us
    dot_general x3, matrix products, contract_rows(): lax.dot_general(weights, rows, (((0,), (0,)), ((), ())), preferred_elemen...  9.2 us
    ppermute x4, waiting for transfers between devices, passed_along(): return lax.ppermute(value, axis, pairs)  7.94 us
    mul x2, other arithmetic, back_norm(): return (grad - unit * jnp.sum(unit * grad, axis=-1, keepdims=True)) * recip  5.77 us
    dot_general x1, matrix products, shards(): jnp.dot(weight_next, txt_next, preferred_element_type=jnp.float32)  4.73 us
    dot_general x1, matrix products, shards(): jnp.dot(weight_prev, txt_prev, preferred_element_type=jnp.float32)  3.68 us
    convert_element_type x1, other arithmetic, shards(): txt_low = unit_txt.astype(jnp.bfloat16)  2.21 us
    dot_general x1, matrix products, shards(): jnp.dot(weight_own, txt_low, preferred_element_type=jnp.float32)  1.86 us
  transfers between devices with their start and end apart: 4, of which 2 were waited for; matrix products, arithmetic and copies ran while one was open for 28% of the time, Pallas kernels for 0%

commit v1 on v0

v1 whole, which is shorter than its diff:
```python
import functools

import jax
import jax.numpy as jnp
from jax import lax
from jax.experimental import pallas as pl
from jax.experimental.pallas import tpu as pltpu
from jax.sharding import PartitionSpec as P

MESH = pl.DeviceIdType.MESH
RING = 8
ROWS = 64
BLOCK = 256
PART = 128


def unit_rows(raw):
    values = raw.astype(jnp.float32)
    recip = lax.rsqrt(jnp.sum(values * values, axis=-1, keepdims=True) + 1e-06)
    return values * recip, recip


def pair_weights(own, some, scale, bias):
    dots = lax.dot_general(own, some, (((1,), (1,)), ((), ())), preferred_element_type=jnp.float32)
    return jax.nn.sigmoid(scale * dots + bias)


def weighted(weights, some):
    return jnp.dot(weights.astype(jnp.bfloat16), some, preferred_element_type=jnp.float32)


def back_norm(raw, recip, grad):
    unit = raw.astype(jnp.float32) * recip
    return (grad - unit * jnp.sum(unit * grad, axis=-1, keepdims=True)) * recip


def exchange(n_blk, n_sub, scale_ref, bias_ref, img, txt, total, raw, low, recips, unit, scalars,
             arrived, load_sem, send_sem, recv_sem, ready_sem):
    count = n_blk * n_sub
    rows = img.shape[0]
    steps = rows // ROWS
    sub = lax.axis_index("sub")
    me = lax.axis_index("blk") * n_sub + sub
    after, before = lax.rem(me + 1, count), lax.rem(me + count - 1, count)
    places = [(at // n_sub, at % n_sub) for at in (after, before)]
    up, down = 0, 1
    spot = lax.rem(sub, RING)

    barrier = pltpu.get_barrier_semaphore()

    @pl.when(spot != RING - 1)
    def _():
        pl.semaphore_signal(barrier, inc=1, device_id=places[up], device_id_type=MESH)

    @pl.when(spot < 2)
    def _():
        pl.semaphore_signal(barrier, inc=1, device_id=places[down], device_id_type=MESH)

    loads = [pltpu.make_async_copy(whole, raw.at[a], load_sem.at[a]) for a, whole in enumerate((img, txt))]
    for load in loads:
        load.start()

    def send(side, k):
        return pltpu.make_async_remote_copy(
            src_ref=(img, txt)[k // steps].at[pl.ds((k % steps) * ROWS, ROWS)],
            dst_ref=arrived.at[side, k],
            send_sem=send_sem.at[side, k],
            recv_sem=recv_sem.at[side, k],
            device_id=places[side],
            device_id_type=MESH,
        )

    def start_sends(side):
        for k in range(2 * steps):
            send(side, k).start()

    @pl.when(spot == RING - 1)
    def _():
        pl.semaphore_wait(barrier, 2)
        pl.semaphore_signal(ready_sem.at[down], inc=1, device_id=places[up], device_id_type=MESH)
        pl.semaphore_signal(ready_sem.at[up], inc=1, device_id=places[down], device_id_type=MESH)
        start_sends(up)
        start_sends(down)

    @pl.when(spot != RING - 1)
    def _():
        pl.semaphore_wait(barrier, 1)

        @pl.when(spot == 0)
        def _():
            start_sends(up)

        @pl.when(spot != 0)
        def _():
            @pl.when(spot > 1)
            def _():
                pl.semaphore_signal(ready_sem.at[up], inc=1, device_id=places[down], device_id_type=MESH)

            start_sends(down)
            pl.semaphore_wait(ready_sem.at[up], 1)
            start_sends(up)

    with jax.named_scope("own_units"):
        for a in range(2):
            loads[a].wait()

            @pl.loop(0, rows // PART)
            def _(m):
                block = pl.ds(pl.multiple_of(m * PART, PART), PART)
                values, recip = unit_rows(raw[a, block])
                low[a, block] = values.astype(jnp.bfloat16)
                recips[a, block] = recip
    scale, bias = scale_ref[0], bias_ref[0]
    scalars[0] = jnp.full(scalars.shape[1:], scale, jnp.float32)
    scalars[1] = jnp.full(scalars.shape[1:], bias, jnp.float32)
    total[...] = jnp.zeros_like(total)

    def add_rows(a, some):
        for m in range(0, rows, BLOCK):
            block = pl.ds(m, BLOCK)
            total[a, block] += weighted(pair_weights(low[a, block], some, scale, bias), some)

    with jax.named_scope("own_pairs"):
        @pl.loop(0, rows // BLOCK)
        def _(j):
            first = pl.multiple_of(j * BLOCK, BLOCK)
            for a in range(2):
                some = low[1 - a, pl.ds(first, BLOCK)]
                for m in range(0, rows, BLOCK):
                    block = pl.ds(m, BLOCK)
                    weights = pair_weights(low[a, block], some, scale, bias)
                    at = lax.broadcasted_iota(jnp.int32, weights.shape, 0) + m
                    to = lax.broadcasted_iota(jnp.int32, weights.shape, 1) + first
                    total[a, block] += weighted(weights - jnp.where(at == to, 1.0, 0.0), some)

    @pl.when(spot == 0)
    def _():
        pl.semaphore_wait(ready_sem.at[down], 1)
        start_sends(down)

    last = 2 * steps - 1

    @pl.loop(0, last + 1)
    def _(k):
        a = 1 - k // steps
        with jax.named_scope("wait"):
            for side in range(2):
                pltpu.make_async_copy(arrived.at[side, k], arrived.at[side, k], recv_sem.at[side, k]).wait()
        with jax.named_scope("step"):
            for side in range(2):
                unit[pl.ds(side * ROWS, ROWS)] = unit_rows(arrived[side, k])[0].astype(jnp.bfloat16)

            @pl.when(k < last)
            def _():
                add_rows(a, unit[...])

            @pl.when(k == steps - 1)
            def _():
                @pl.loop(0, rows // PART)
                def _(m):
                    block = pl.ds(pl.multiple_of(m * PART, PART), PART)
                    total[1, block] = back_norm(raw[1, block], recips[1, block], scale * total[1, block])

    with jax.named_scope("wait_sends"):
        for k in range(2 * steps):
            for side in range(2):
                send(side, k).wait_send()


def complete(total, raw, low, recips, unit, scalars, g_img, g_txt, result, out_sem):
    rows = result.shape[0]
    whole = pltpu.make_async_copy(total.at[1], g_txt, out_sem.at[rows // PART])
    whole.start()
    scale, bias = scalars[0, 0:1, 0:1], scalars[1, 0:1, 0:1]
    some = unit[...]
    outs = []
    for m in range(rows // PART):
        block = pl.ds(m * PART, PART)
        grad = total[0, block] + weighted(pair_weights(low[0, block], some, scale, bias), some)
        result[block] = back_norm(raw[0, block], recips[0, block], scale * grad)
        outs.append(pltpu.make_async_copy(result.at[block], g_img.at[block], out_sem.at[m]))
        outs[-1].start()
    for out in outs:
        out.wait()
    whole.wait()


def solution(mesh):
    n_blk, n_sub = mesh.shape["blk"], mesh.shape["sub"]

    def step(images, texts, logit_scale, logit_bias):
        rows, width = images.shape
        steps = rows // ROWS
        vmem = pl.BlockSpec(memory_space=pltpu.VMEM)
        hbm = pl.BlockSpec(memory_space=pltpu.HBM)
        args = [logit_scale, logit_bias] + [pltpu.with_memory_space_constraint(x, pltpu.HBM) for x in (images, texts)]
        smem = pl.BlockSpec(memory_space=pltpu.SMEM)
        held = pl.pallas_call(
            functools.partial(exchange, n_blk, n_sub),
            out_shape=[
                jax.ShapeDtypeStruct((2, rows, width), jnp.float32),
                jax.ShapeDtypeStruct((2, rows, width), jnp.bfloat16),
                jax.ShapeDtypeStruct((2, rows, width), jnp.bfloat16),
                jax.ShapeDtypeStruct((2, rows, 1), jnp.float32),
                jax.ShapeDtypeStruct((2 * ROWS, width), jnp.bfloat16),
                jax.ShapeDtypeStruct((2, 8, 128), jnp.float32),
            ],
            in_specs=[smem] * 2 + [hbm] * 2,
            out_specs=[vmem] * 6,
            scratch_shapes=[
                pltpu.VMEM((2, 2 * steps, ROWS, width), jnp.bfloat16),
                pltpu.SemaphoreType.DMA((2,)),
                pltpu.SemaphoreType.DMA((2, 2 * steps)),
                pltpu.SemaphoreType.DMA((2, 2 * steps)),
                pltpu.SemaphoreType.REGULAR((2,)),
            ],
            compiler_params=pltpu.CompilerParams(
                collective_id=0, has_side_effects=True, vmem_limit_bytes=24 << 20
            ),
        )(*args)
        return pl.pallas_call(
            complete,
            out_shape=[jax.ShapeDtypeStruct((rows, width), jnp.float32)] * 2,
            in_specs=[vmem] * 6,
            out_specs=[hbm] * 2,
            scratch_shapes=[
                pltpu.VMEM((rows, width), jnp.float32),
                pltpu.SemaphoreType.DMA((rows // PART + 1,)),
            ],
            compiler_params=pltpu.CompilerParams(vmem_limit_bytes=24 << 20),
        )(*held)

    rows_spec = P(("blk", "sub"), None)
    return jax.shard_map(
        step, mesh=mesh, in_specs=(rows_spec, rows_spec, P(), P()), out_specs=(rows_spec, rows_spec), check_vma=False
    )
```

time: 70.4 us -> 53.2 us (0.76)
  Pallas kernels: 0 us -> 51.1 us
  starting transfers between devices: 29 us -> 0 us
  matrix products: 20.3 us -> 0 us
  other arithmetic: 10.7 us -> 0 us
  waiting for transfers between devices: 7.94 us -> 0 us
    pallas_call x0 -> x2, Pallas kernels: none -> 51.1 us  [the longest x1 49.2 us: step(): pl.pallas_call(functools.partial(exchange, n_blk, n_sub), out_shape=[jax....]
    ppermute x4 -> x0, starting transfers between devices: 29 us -> none  [passed_along(): return lax.ppermute(value, axis, pairs)]
    dot_general x7 -> x0, matrix products: 20.3 us -> none  [the longest x3 9.2 us: contract_rows(): lax.dot_general(weights, rows, (((0,), (0,)), ((), ())), preferred_elemen...]
    ppermute x4 -> x0, waiting for transfers between devices: 7.94 us -> none  [passed_along(): return lax.ppermute(value, axis, pairs)]
    mul x2 -> x0, other arithmetic: 5.77 us -> none  [back_norm(): return (grad - unit * jnp.sum(unit * grad, axis=-1, keepdims=True)) * recip]
    convert_element_type x2 -> x0, other arithmetic: 3.3 us -> none  [the longest x1 2.21 us: shards(): txt_low = unit_txt.astype(jnp.bfloat16)]
    reduce_sum x2 -> x0, other arithmetic: 1.66 us -> none  [unit_rows(): recip = lax.rsqrt(jnp.sum(values * values, axis=-1, keepdims=True) + 1e-06)]
  transfers between devices with their start and end apart: 4 -> 0, of which waited for: 2 -> 0; matrix products, arithmetic and copies ran while one was open for 28% -> 0% of each run, Pallas kernels for 0% -> 0%
where the time goes in v1:
time: 53.2 us; the launch traced here: 53 us
  Pallas kernels  51.1 us (96%)
  between operations  1.93 us (4%)
    pallas_call x1, Pallas kernels, step(): pl.pallas_call(functools.partial(exchange, n_blk, n_sub), out_shape=[jax....  49.2 us
    pallas_call x1, Pallas kernels, step(): pl.pallas_call(complete, out_shape=[jax.ShapeDtypeStruct((rows, width), j...  1.94 us

profile of v1, /device:TPU:6, one launch (start us, length us, event | category | flops | bytes accessed | tf_op | source)
XLA Modules:
  0.0 53.0 jit_solution(15899055825207303118)
XLA Ops:
  1.9 49.2 %shard_map.59 = (f32[2,512,768]{2,1,0:T(8,128)S(1)}, bf16[2,512,768]{2,1,0:T(8,128)(2,1)S(1)}, bf16[2,512,768]{2,1,0:T(8,128)(2,1)S(1)}, f32[2,512,1]{2,1,0:T(8,...) custom-call(f32[1]{0:T(128)S(6)} %copy.6.scale_ref, f32[1]{0:T(128)S(6)} %copy.7.bias_ref, ...), custom_call_target="tpu_custom_call" | custom-call | tf_op jit(solution)/shard_map/pallas_call | solution.py:198
  51.1 1.9 %shard_map.60 = (f32[512,768]{1,0:T(8,128)}, f32[512,768]{1,0:T(8,128)}) custom-call(f32[2,512,768]{2,1,0:T(8,128)S(1)} %get-tuple-element.8.total, bf16[2,512,768]{2,1,0:T(8,128)(2,1)S(1)} %get-tuple-element.9.raw, bf16[2,512,768]{2,1,0:T(8,128)(2,1)S(1)} %get-tuple-element.10.low, f32[2,512,1]{2,1,0:T(8,128)S(1)} %get-tuple-element.11.recips, ...), custom_call_target="tpu_custom_call" | custom-call | tf_op jit(solution)/shard_map/pallas_call | solution.py:221

commit v2 on v1

v2 whole, which is shorter than its diff:
```python
import functools

import jax
import jax.numpy as jnp
from jax import lax
from jax.experimental import pallas as pl
from jax.experimental.pallas import tpu as pltpu
from jax.sharding import PartitionSpec as P

MESH = pl.DeviceIdType.MESH
RING = 8
ROWS = 128
SMALL = 64
RELAYED = (2, 4)
BLOCK = 256
PART = 128


def unit_rows(raw):
    values = raw.astype(jnp.float32)
    recip = lax.rsqrt(jnp.sum(values * values, axis=-1, keepdims=True) + 1e-06)
    return values * recip, recip


def pair_weights(own, some, scale, bias):
    dots = lax.dot_general(own, some, (((1,), (1,)), ((), ())), preferred_element_type=jnp.float32)
    return jax.nn.sigmoid(scale * dots + bias)


def weighted(weights, some):
    return jnp.dot(weights.astype(jnp.bfloat16), some, preferred_element_type=jnp.float32)


def back_norm(raw, recip, grad):
    unit = raw.astype(jnp.float32) * recip
    return (grad - unit * jnp.sum(unit * grad, axis=-1, keepdims=True)) * recip


def exchange(n_blk, n_sub, scale_ref, bias_ref, img, txt, total, raw, low, recips, final, scalars,
             arrived, unit, passing, load_sem, send_sem, recv_sem, ready_sem, relay_sem):
    count = n_blk * n_sub
    rows = img.shape[0]
    steps = rows // ROWS
    blk, sub = lax.axis_index("blk"), lax.axis_index("sub")
    me = blk * n_sub + sub
    after, before = lax.rem(me + 1, count), lax.rem(me + count - 1, count)
    places = [(at // n_sub, at % n_sub) for at in (after, before)]
    up, down = 0, 1
    spot = lax.rem(sub, RING)
    core, part = lax.rem(blk, 2), lax.rem(blk // 2, 3)
    first = sub == 0
    early = first & ((core == 1) | (part == 0))
    yields = [first & (core == 1) & (part == 2), first & (core == 0) & (part != 0)]
    sender = (core == 1) & (part == 2) & (sub == n_sub - 1) & (blk != n_blk - 1)
    relays = [
        (core == 1) & (part == 0) & (sub == RING) & (blk != 1),
        (core == 1) & (part == 2) & (sub == 2 * RING) & (blk != n_blk - 1),
    ]
    taker = first & (core == 0) & (part == 0) & (blk != 0)
    relay = relays[0] | relays[1]
    sender_place = (jnp.where(relays[0], blk - 2, blk), n_sub - 1)
    relay_places = [(blk + 2, RING), (blk, 2 * RING)]
    taker_place = (jnp.where(relays[0], blk - 1, blk + 1), 0)
    taken_places = [(blk + 1, RING), (blk - 1, 2 * RING)]
    pieces = [(k * ROWS, ROWS) for k in range(2 * steps - 1)]
    pieces += [(2 * rows - 2 * SMALL, SMALL), (2 * rows - SMALL, SMALL)]

    barrier = pltpu.get_barrier_semaphore()

    @pl.when(spot != RING - 1)
    def _():
        pl.semaphore_signal(barrier, inc=1, device_id=places[up], device_id_type=MESH)

    @pl.when(spot < 2)
    def _():
        pl.semaphore_signal(barrier, inc=1, device_id=places[down], device_id_type=MESH)

    @pl.when(relay)
    def _():
        pl.semaphore_signal(barrier, inc=1, device_id=sender_place, device_id_type=MESH)

    @pl.when(taker)
    def _():
        for place in taken_places:
            pl.semaphore_signal(barrier, inc=1, device_id=place, device_id_type=MESH)

    loads = [pltpu.make_async_copy(whole, raw.at[a], load_sem.at[a]) for a, whole in enumerate((img, txt))]
    for load in loads:
        load.start()

    def send(side, k, dst, recv, place):
        at, size = pieces[k]
        pltpu.make_async_remote_copy(
            src_ref=(img, txt)[at // rows].at[pl.ds(at % rows, size)],
            dst_ref=dst,
            send_sem=send_sem.at[side],
            recv_sem=recv,
            device_id=place,
            device_id_type=MESH,
        ).start()

    def start_sends(side, skipped=(), begin=0, end=len(pieces)):
        for k, piece in list(enumerate(pieces))[begin:end]:
            if k not in skipped:
                send(side, k, arrived.at[side, pl.ds(*piece)], recv_sem.at[side, k], places[side])

    def onward(k):
        return pltpu.make_async_remote_copy(
            src_ref=passing,
            dst_ref=arrived.at[up, pl.ds(*pieces[k])],
            send_sem=relay_sem.at[1],
            recv_sem=recv_sem.at[up, k],
            device_id=taker_place,
            device_id_type=MESH,
        )

    def answered_sends(end=len(pieces)):
        pl.semaphore_wait(ready_sem.at[down], 1)
        start_sends(down, end=end)

    @pl.when(spot == RING - 1)
    def _():
        pl.semaphore_wait(barrier, jnp.where(sender, 2 + len(RELAYED), 2))
        pl.semaphore_signal(ready_sem.at[down], inc=1, device_id=places[up], device_id_type=MESH)
        pl.semaphore_signal(ready_sem.at[up], inc=1, device_id=places[down], device_id_type=MESH)

        @pl.when(sender)
        def _():
            send(up, RELAYED[0], passing, relay_sem.at[0], relay_places[0])
            start_sends(up, RELAYED, 0, 1)
            send(up, RELAYED[1], passing, relay_sem.at[0], relay_places[1])
            start_sends(up, RELAYED, 1)

        @pl.when(jnp.logical_not(sender))
        def _():
            start_sends(up)

        start_sends(down)

    @pl.when(spot != RING - 1)
    def _():
        pl.semaphore_wait(barrier, jnp.where(relay, 2, 1))

        @pl.when(spot == 0)
        def _():
            start_sends(up)

        @pl.when(spot != 0)
        def _():
            @pl.when(spot > 1)
            def _():
                pl.semaphore_signal(ready_sem.at[up], inc=1, device_id=places[down], device_id_type=MESH)

            start_sends(down)
            pl.semaphore_wait(ready_sem.at[up], 1)
            start_sends(up)

    with jax.named_scope("own_units"):
        for a in range(2):
            loads[a].wait()

            @pl.loop(0, rows // PART)
            def _(m):
                block = pl.ds(pl.multiple_of(m * PART, PART), PART)
                values, recip = unit_rows(raw[a, block])
                low[a, block] = values.astype(jnp.bfloat16)
                recips[a, block] = recip
    pl.when((spot == 0) & jnp.logical_not(early | relays[0] | yields[1]))(answered_sends)
    pl.when(relays[0])(lambda: answered_sends(5))
    pl.when(yields[1])(lambda: answered_sends(4))
    scale, bias = scale_ref[0], bias_ref[0]
    scalars[0] = jnp.full(scalars.shape[1:], scale, jnp.float32)
    scalars[1] = jnp.full(scalars.shape[1:], bias, jnp.float32)
    total[...] = jnp.zeros_like(total)

    def add_rows(a, some):
        blocks = [pl.ds(m, BLOCK) for m in range(0, rows, BLOCK)]
        weights = [pair_weights(low[a, block], some, scale, bias).astype(jnp.bfloat16) for block in blocks]
        for block, part in zip(blocks, weights):
            total[a, block] += weighted(part, some)

    with jax.named_scope("own_pairs"):
        @pl.loop(0, rows // BLOCK)
        def _(j):
            begin = pl.multiple_of(j * BLOCK, BLOCK)
            for a in range(2):
                some = low[1 - a, pl.ds(begin, BLOCK)]
                for m in range(0, rows, BLOCK):
                    block = pl.ds(m, BLOCK)
                    weights = pair_weights(low[a, block], some, scale, bias)
                    at = lax.broadcasted_iota(jnp.int32, weights.shape, 0) + m
                    to = lax.broadcasted_iota(jnp.int32, weights.shape, 1) + begin
                    total[a, block] += weighted(weights - jnp.where(at == to, 1.0, 0.0), some)

    pl.when(early & jnp.logical_not(yields[0]))(answered_sends)
    pl.when(yields[0])(lambda: answered_sends(3))

    def receive(k, at, size, into):
        for side in range(2):
            there = arrived.at[side, pl.ds(at, size)]
            with jax.named_scope("wait"):
                pltpu.make_async_copy(there, there, recv_sem.at[side, k]).wait()
            into[pl.ds(side * size, size)] = unit_rows(there[...])[0].astype(jnp.bfloat16)

    @pl.loop(0, 2 * steps - 1)
    def _(k):
        receive(k, pl.multiple_of(k * ROWS, ROWS), ROWS, unit)
        with jax.named_scope("step"):
            add_rows(1 - k // steps, unit[...])

        pl.when(yields[0] & (k == 3))(lambda: start_sends(down, begin=3))
        pl.when(yields[1] & (k == 3))(lambda: start_sends(down, begin=4))

        def pass_on(m):
            pltpu.make_async_copy(passing, passing, relay_sem.at[0]).wait()
            onward(RELAYED[m]).start()

        @pl.when(relays[0] & (k == 3))
        def _():
            pass_on(0)
            start_sends(down, begin=5)

        pl.when(relays[1] & (k == 1))(lambda: pass_on(1))

        @pl.when(k == steps - 1)
        def _():
            @pl.loop(0, rows // PART)
            def _(m):
                block = pl.ds(pl.multiple_of(m * PART, PART), PART)
                total[1, block] = back_norm(raw[1, block], recips[1, block], scale * total[1, block])


    k = 2 * steps - 1
    receive(k, *pieces[k], unit)
    with jax.named_scope("small"):
        add_rows(0, unit[: 2 * SMALL])
    receive(k + 1, *pieces[k + 1], final)
    with jax.named_scope("wait_sends"):
        for side in range(2):
            pltpu.make_async_copy(arrived.at[side], arrived.at[side], send_sem.at[side]).wait()
    pl.when(relay)(onward(RELAYED[0]).wait_send)


def complete(total, raw, low, recips, final, scalars, g_img, g_txt, result, out_sem):
    rows = result.shape[0]
    whole = pltpu.make_async_copy(total.at[1], g_txt, out_sem.at[rows // PART])
    whole.start()
    scale, bias = scalars[0, 0:1, 0:1], scalars[1, 0:1, 0:1]
    some = final[...]
    outs = [whole]
    for at in range(0, rows, BLOCK):
        weights = pair_weights(low[0, pl.ds(at, BLOCK)], some, scale, bias)
        for m in range(at // PART, (at + BLOCK) // PART):
            block = pl.ds(m * PART, PART)
            grad = total[0, block] + weighted(weights[m * PART - at : (m + 1) * PART - at], some)
            result[block] = back_norm(raw[0, block], recips[0, block], scale * grad)
            outs.append(pltpu.make_async_copy(result.at[block], g_img.at[block], out_sem.at[m]))
            outs[-1].start()
    for out in outs:
        out.wait()


def solution(mesh):
    n_blk, n_sub = mesh.shape["blk"], mesh.shape["sub"]

    def step(images, texts, logit_scale, logit_bias):
        rows, width = images.shape
        steps = rows // ROWS
        vmem = pl.BlockSpec(memory_space=pltpu.VMEM)
        hbm = pl.BlockSpec(memory_space=pltpu.HBM)
        args = [logit_scale, logit_bias] + [pltpu.with_memory_space_constraint(x, pltpu.HBM) for x in (images, texts)]
        smem = pl.BlockSpec(memory_space=pltpu.SMEM)
        held = pl.pallas_call(
            functools.partial(exchange, n_blk, n_sub),
            out_shape=[
                jax.ShapeDtypeStruct((2, rows, width), jnp.float32),
                jax.ShapeDtypeStruct((2, rows, width), jnp.bfloat16),
                jax.ShapeDtypeStruct((2, rows, width), jnp.bfloat16),
                jax.ShapeDtypeStruct((2, rows, 1), jnp.float32),
                jax.ShapeDtypeStruct((2 * SMALL, width), jnp.bfloat16),
                jax.ShapeDtypeStruct((2, 8, 128), jnp.float32),
            ],
            in_specs=[smem] * 2 + [hbm] * 2,
            out_specs=[vmem] * 6,
            scratch_shapes=[
                pltpu.VMEM((2, 2 * rows, width), jnp.bfloat16),
                pltpu.VMEM((2 * ROWS, width), jnp.bfloat16),
                pltpu.VMEM((ROWS, width), jnp.bfloat16),
                pltpu.SemaphoreType.DMA((2,)),
                pltpu.SemaphoreType.DMA((2,)),
                pltpu.SemaphoreType.DMA((2, 2 * steps + 1)),
                pltpu.SemaphoreType.REGULAR((2,)),
                pltpu.SemaphoreType.DMA((2,)),
            ],
            compiler_params=pltpu.CompilerParams(
                collective_id=0, has_side_effects=True, vmem_limit_bytes=24 << 20
            ),
        )(*args)
        return pl.pallas_call(
            complete,
            out_shape=[jax.ShapeDtypeStruct((rows, width), jnp.float32)] * 2,
            in_specs=[vmem] * 6,
            out_specs=[hbm] * 2,
            scratch_shapes=[
                pltpu.VMEM((rows, width), jnp.float32),
                pltpu.SemaphoreType.DMA((rows // PART + 1,)),
            ],
            compiler_params=pltpu.CompilerParams(vmem_limit_bytes=24 << 20),
        )(*held)

    rows_spec = P(("blk", "sub"), None)
    return jax.shard_map(
        step, mesh=mesh, in_specs=(rows_spec, rows_spec, P(), P()), out_specs=(rows_spec, rows_spec), check_vma=False
    )
```

time: 53.2 us -> 47.4 us (0.89)
  Pallas kernels: 51.1 us -> 45 us
    pallas_call x1, Pallas kernels: 49.2 us -> 43 us  [step(): pl.pallas_call(functools.partial(exchange, n_blk, n_sub), out_shape=[jax....]
where the time goes in v2:
time: 47.4 us; the launch traced here: 46.9 us
  Pallas kernels  45 us (95%)
  between operations  1.93 us (4%)
    pallas_call x1, Pallas kernels, step(): pl.pallas_call(functools.partial(exchange, n_blk, n_sub), out_shape=[jax....  43 us
    pallas_call x1, Pallas kernels, step(): pl.pallas_call(complete, out_shape=[jax.ShapeDtypeStruct((rows, width), j...  2.04 us

profile of v2, /device:TPU:6, one launch (start us, length us, event | category | flops | bytes accessed | tf_op | source)
XLA Modules:
  0.0 46.9 jit_solution(14190039154661204305)
XLA Ops:
  1.9 43.0 %shard_map.59 = (f32[2,512,768]{2,1,0:T(8,128)S(1)}, bf16[2,512,768]{2,1,0:T(8,128)(2,1)S(1)}, bf16[2,512,768]{2,1,0:T(8,128)(2,1)S(1)}, f32[2,512,1]{2,1,0:T(8,...) custom-call(f32[1]{0:T(128)S(6)} %copy.6.scale_ref, f32[1]{0:T(128)S(6)} %copy.7.bias_ref, ...), custom_call_target="tpu_custom_call" | custom-call | tf_op jit(solution)/shard_map/pallas_call | solution.py:273
  44.9 2.0 %shard_map.60 = (f32[512,768]{1,0:T(8,128)}, f32[512,768]{1,0:T(8,128)}) custom-call(f32[2,512,768]{2,1,0:T(8,128)S(1)} %get-tuple-element.8.total, bf16[2,512,768]{2,1,0:T(8,128)(2,1)S(1)} %get-tuple-element.9.raw, bf16[2,512,768]{2,1,0:T(8,128)(2,1)S(1)} %get-tuple-element.10.low, f32[2,512,1]{2,1,0:T(8,128)S(1)} %get-tuple-element.11.recips, ...), custom_call_target="tpu_custom_call" | custom-call | tf_op jit(solution)/shard_map/pallas_call | solution.py:299

commit v3 on v2

--- a/solution.py
+++ b/solution.py
@@ -38,20 +38,23 @@
 
 def exchange(n_blk, n_sub, scale_ref, bias_ref, img, txt, total, raw, low, recips, final, scalars,
              arrived, unit, passing, load_sem, send_sem, recv_sem, ready_sem, relay_sem):
-    count = n_blk * n_sub
     rows = img.shape[0]
     steps = rows // ROWS
     blk, sub = lax.axis_index("blk"), lax.axis_index("sub")
-    me = blk * n_sub + sub
-    after, before = lax.rem(me + 1, count), lax.rem(me + count - 1, count)
-    places = [(at // n_sub, at % n_sub) for at in (after, before)]
+    first, ended = sub == 0, sub == n_sub - 1
+    next_blk, last_blk = jnp.where(blk == n_blk - 1, 0, blk + 1), jnp.where(blk == 0, n_blk - 1, blk - 1)
+    places = [
+        (jnp.where(ended, next_blk, blk), jnp.where(ended, 0, sub + 1)),
+        (jnp.where(first, last_blk, blk), jnp.where(first, n_sub - 1, sub - 1)),
+    ]
     up, down = 0, 1
     spot = lax.rem(sub, RING)
-    core, part = lax.rem(blk, 2), lax.rem(blk // 2, 3)
-    first = sub == 0
+    pair, core = blk // 2, blk % 2
+    part = pair - (pair * 11 // 32) * 3
     early = first & ((core == 1) | (part == 0))
     yields = [first & (core == 1) & (part == 2), first & (core == 0) & (part != 0)]
-    sender = (core == 1) & (part == 2) & (sub == n_sub - 1) & (blk != n_blk - 1)
+    near = ended & (core == 1) & (part != 2)
+    sender = ended & (core == 1) & (part == 2) & (blk != n_blk - 1)
     relays = [
         (core == 1) & (part == 0) & (sub == RING) & (blk != 1),
         (core == 1) & (part == 2) & (sub == 2 * RING) & (blk != n_blk - 1),
@@ -67,7 +70,7 @@
 
     barrier = pltpu.get_barrier_semaphore()
 
-    @pl.when(spot != RING - 1)
+    @pl.when((spot != RING - 1) | near)
     def _():
         pl.semaphore_signal(barrier, inc=1, device_id=places[up], device_id_type=MESH)
 
@@ -85,9 +88,6 @@
             pl.semaphore_signal(barrier, inc=1, device_id=place, device_id_type=MESH)
 
     loads = [pltpu.make_async_copy(whole, raw.at[a], load_sem.at[a]) for a, whole in enumerate((img, txt))]
-    for load in loads:
-        load.start()
-
     def send(side, k, dst, recv, place):
         at, size = pieces[k]
         pltpu.make_async_remote_copy(
@@ -121,7 +121,11 @@
     @pl.when(spot == RING - 1)
     def _():
         pl.semaphore_wait(barrier, jnp.where(sender, 2 + len(RELAYED), 2))
-        pl.semaphore_signal(ready_sem.at[down], inc=1, device_id=places[up], device_id_type=MESH)
+
+        @pl.when(jnp.logical_not(near))
+        def _():
+            pl.semaphore_signal(ready_sem.at[down], inc=1, device_id=places[up], device_id_type=MESH)
+
         pl.semaphore_signal(ready_sem.at[up], inc=1, device_id=places[down], device_id_type=MESH)
 
         @pl.when(sender)
@@ -139,11 +143,12 @@
 
     @pl.when(spot != RING - 1)
     def _():
-        pl.semaphore_wait(barrier, jnp.where(relay, 2, 1))
+        pl.semaphore_wait(barrier, jnp.where(relay | yields[1], 2, 1))
 
         @pl.when(spot == 0)
         def _():
             start_sends(up)
+            pl.when(yields[1])(lambda: start_sends(down, end=4))
 
         @pl.when(spot != 0)
         def _():
@@ -154,6 +159,9 @@
             start_sends(down)
             pl.semaphore_wait(ready_sem.at[up], 1)
             start_sends(up)
+
+    for load in loads:
+        load.start()
 
     with jax.named_scope("own_units"):
         for a in range(2):
@@ -167,7 +175,6 @@
                 recips[a, block] = recip
     pl.when((spot == 0) & jnp.logical_not(early | relays[0] | yields[1]))(answered_sends)
     pl.when(relays[0])(lambda: answered_sends(5))
-    pl.when(yields[1])(lambda: answered_sends(4))
     scale, bias = scale_ref[0], bias_ref[0]
     scalars[0] = jnp.full(scalars.shape[1:], scale, jnp.float32)
     scalars[1] = jnp.full(scalars.shape[1:], bias, jnp.float32)
@@ -202,25 +209,25 @@
                 pltpu.make_async_copy(there, there, recv_sem.at[side, k]).wait()
             into[pl.ds(side * size, size)] = unit_rows(there[...])[0].astype(jnp.bfloat16)
 
+    def pass_on(m):
+        pltpu.make_async_copy(passing, passing, relay_sem.at[0]).wait()
+        onward(RELAYED[m]).start()
+
     @pl.loop(0, 2 * steps - 1)
     def _(k):
         receive(k, pl.multiple_of(k * ROWS, ROWS), ROWS, unit)
+        pl.when(yields[0] & (k == 3))(lambda: start_sends(down, begin=3))
+        pl.when(yields[1] & (k == 3))(lambda: start_sends(down, begin=4))
+
+        @pl.when(relays[0] & (k == 3))
+        def _():
+            pass_on(0)
+            start_sends(down, begin=5)
+
+        pl.when(relays[1] & (k == 1))(lambda: pass_on(1))
+
         with jax.named_scope("step"):
             add_rows(1 - k // steps, unit[...])
-
-        pl.when(yields[0] & (k == 3))(lambda: start_sends(down, begin=3))
-        pl.when(yields[1] & (k == 3))(lambda: start_sends(down, begin=4))
-
-        def pass_on(m):
-            pltpu.make_async_copy(passing, passing, relay_sem.at[0]).wait()
-            onward(RELAYED[m]).start()
-
-        @pl.when(relays[0] & (k == 3))
-        def _():
-            pass_on(0)
-            start_sends(down, begin=5)
-
-        pl.when(relays[1] & (k == 1))(lambda: pass_on(1))
 
         @pl.when(k == steps - 1)
         def _():

time: 47.4 us -> 47.4 us (level)
  no operation moved by 1% of the time
where the time goes in v3:
time: 47.4 us; the launch traced here: 47 us
  Pallas kernels  45 us (95%)
  between operations  1.93 us (4%)
    pallas_call x1, Pallas kernels, step(): pl.pallas_call(functools.partial(exchange, n_blk, n_sub), out_shape=[jax....  43 us
    pallas_call x1, Pallas kernels, step(): pl.pallas_call(complete, out_shape=[jax.ShapeDtypeStruct((rows, width), j...  2.04 us

profile of v3, /device:TPU:6, one launch (start us, length us, event | category | flops | bytes accessed | tf_op | source)
XLA Modules:
  0.0 47.0 jit_solution(3000692156810010018)
XLA Ops:
  1.9 43.0 %shard_map.59 = (f32[2,512,768]{2,1,0:T(8,128)S(1)}, bf16[2,512,768]{2,1,0:T(8,128)(2,1)S(1)}, bf16[2,512,768]{2,1,0:T(8,128)(2,1)S(1)}, f32[2,512,1]{2,1,0:T(8,...) custom-call(f32[1]{0:T(128)S(6)} %copy.6.scale_ref, f32[1]{0:T(128)S(6)} %copy.7.bias_ref, ...), custom_call_target="tpu_custom_call" | custom-call | tf_op jit(solution)/shard_map/pallas_call | solution.py:280
  44.9 2.0 %shard_map.60 = (f32[512,768]{1,0:T(8,128)}, f32[512,768]{1,0:T(8,128)}) custom-call(f32[2,512,768]{2,1,0:T(8,128)S(1)} %get-tuple-element.8.total, bf16[2,512,768]{2,1,0:T(8,128)(2,1)S(1)} %get-tuple-element.9.raw, bf16[2,512,768]{2,1,0:T(8,128)(2,1)S(1)} %get-tuple-element.10.low, f32[2,512,1]{2,1,0:T(8,128)S(1)} %get-tuple-element.11.recips, ...), custom_call_target="tpu_custom_call" | custom-call | tf_op jit(solution)/shard_map/pallas_call | solution.py:306

commit v4 on v3

--- a/solution.py
+++ b/solution.py
@@ -255,14 +255,12 @@
     scale, bias = scalars[0, 0:1, 0:1], scalars[1, 0:1, 0:1]
     some = final[...]
     outs = [whole]
-    for at in range(0, rows, BLOCK):
-        weights = pair_weights(low[0, pl.ds(at, BLOCK)], some, scale, bias)
-        for m in range(at // PART, (at + BLOCK) // PART):
-            block = pl.ds(m * PART, PART)
-            grad = total[0, block] + weighted(weights[m * PART - at : (m + 1) * PART - at], some)
-            result[block] = back_norm(raw[0, block], recips[0, block], scale * grad)
-            outs.append(pltpu.make_async_copy(result.at[block], g_img.at[block], out_sem.at[m]))
-            outs[-1].start()
+    for m in range(rows // PART):
+        block = pl.ds(m * PART, PART)
+        grad = total[0, block] + weighted(pair_weights(low[0, block], some, scale, bias), some)
+        result[block] = back_norm(raw[0, block], recips[0, block], scale * grad)
+        outs.append(pltpu.make_async_copy(result.at[block], g_img.at[block], out_sem.at[m]))
+        outs[-1].start()
     for out in outs:
         out.wait()
 

time: 47.4 us -> 47.3 us (level)
  no operation moved by 1% of the time
where the time goes in v4:
time: 47.3 us; the launch traced here: 46.9 us
  Pallas kernels  44.9 us (95%)
  between operations  1.93 us (4%)
    pallas_call x1, Pallas kernels, step(): pl.pallas_call(functools.partial(exchange, n_blk, n_sub), out_shape=[jax....  43 us
    pallas_call x1, Pallas kernels, step(): pl.pallas_call(complete, out_shape=[jax.ShapeDtypeStruct((rows, width), j...  1.94 us

profile of v4, /device:TPU:6, one launch (start us, length us, event | category | flops | bytes accessed | tf_op | source)
XLA Modules:
  0.0 46.9 jit_solution(11565428274497430172)
XLA Ops:
  1.9 43.0 %shard_map.59 = (f32[2,512,768]{2,1,0:T(8,128)S(1)}, bf16[2,512,768]{2,1,0:T(8,128)(2,1)S(1)}, bf16[2,512,768]{2,1,0:T(8,128)(2,1)S(1)}, f32[2,512,1]{2,1,0:T(8,...) custom-call(f32[1]{0:T(128)S(6)} %copy.6.scale_ref, f32[1]{0:T(128)S(6)} %copy.7.bias_ref, ...), custom_call_target="tpu_custom_call" | custom-call | tf_op jit(solution)/shard_map/pallas_call | solution.py:278
  44.9 1.9 %shard_map.60 = (f32[512,768]{1,0:T(8,128)}, f32[512,768]{1,0:T(8,128)}) custom-call(f32[2,512,768]{2,1,0:T(8,128)S(1)} %get-tuple-element.8.total, bf16[2,512,768]{2,1,0:T(8,128)(2,1)S(1)} %get-tuple-element.9.raw, bf16[2,512,768]{2,1,0:T(8,128)(2,1)S(1)} %get-tuple-element.10.low, f32[2,512,1]{2,1,0:T(8,128)S(1)} %get-tuple-element.11.recips, ...), custom_call_target="tpu_custom_call" | custom-call | tf_op jit(solution)/shard_map/pallas_call | solution.py:304
